TPU v7x, 32 devices: a whole 2x2x4 slice. The times are simulated.
32 devices in a mesh: row: 4 (over x, core), col: 8 (over z, y).
Axes of the slice: x: 2, y: 2, z: 4, core: 2. Of those that a mesh axis runs over, the one named last changes fastest.
Arguments:
- kernel: bfloat16 [32768, 32768], P('row', 'col'), may hold values from -1 to 1
- random_cols: bfloat16 [32768, 256], P('row'), may hold values from -6 to 6
- tree_perm: int32 [32768], replicated, may hold values from 0 to 32767, as said below
- leaf_units: int32 [32], replicated, may hold values from 1 to 8, 160 in all
Outputs:
- bases: bfloat16 [4, 32768, 256], P(None, ('row', 'col'))
Inputs may be any that keep to these rules, and one draw needn't show every extreme that they name: `tree_perm`: A permutation. Cut tree positions and stored rows alike into blocks of 1024 in order: every tree block takes at most 32 rows from any one stored block, some pair of blocks shares exactly 32, and every stored block gives 1024 rows in all. `leaf_units`: they sum to 160.
All inputs are finite; a program needn't handle non-finite values.
Results may differ from a plain program's by a relative error of at most 0.0067.
Values may be sent and summed in bfloat16 or wider, within the bound.
A program may use at most 192 MiB of HBM per device.

v0:
```python
import jax
import jax.numpy as jnp
from jax import lax
from jax.sharding import PartitionSpec as P

UNIT = 128
MINU = 4
LEVELS = 3


def shards(kernel, random_cols, tree_perm, leaf_units):
    width = random_cols.shape[1]
    partial_w = lax.dot_general(
        kernel, random_cols, (((0,), (0,)), ((), ())), preferred_element_type=jnp.float32
    )
    sample_w = lax.psum(partial_w, "row").astype(jnp.bfloat16)
    columns_count = lax.axis_size("col")
    rows_dev = kernel.shape[0] // columns_count
    sample = lax.psum_scatter(
        jnp.dot(kernel, sample_w, preferred_element_type=jnp.float32),
        "col",
        scatter_dimension=0,
        tiled=True,
    ).astype(jnp.bfloat16)
    devices = lax.axis_size("row") * columns_count
    total_rows = tree_perm.shape[0]
    device = lax.axis_index(("row", "col"))
    offset = device * rows_dev
    wanted = lax.dynamic_slice_in_dim(tree_perm, offset, rows_dev)
    inverse = (
        jnp.zeros((total_rows,), jnp.int32)
        .at[tree_perm]
        .set(jnp.arange(total_rows, dtype=jnp.int32))
    )
    placed = lax.dynamic_slice_in_dim(inverse, offset, rows_dev)
    capacity = (rows_dev + devices - 1) // devices
    target = placed // rows_dev
    ahead_mine = (target[None, :] == target[:, None]) & (placed[None, :] < placed[:, None])
    slot = target * capacity + jnp.sum(ahead_mine, axis=1)
    outgoing = jnp.zeros((devices * capacity, width), jnp.bfloat16).at[slot].set(sample)
    incoming = lax.all_to_all(outgoing, ("row", "col"), split_axis=0, concat_axis=0, tiled=True)
    source = wanted // rows_dev
    order = jnp.arange(rows_dev, dtype=jnp.int32)
    ahead_theirs = (source[None, :] == source[:, None]) & (order[None, :] < order[:, None])
    pick = source * capacity + jnp.sum(ahead_theirs, axis=1)
    tree_rows = jnp.take(incoming, pick, axis=0)
    sizes = UNIT * (MINU - 1 + leaf_units)
    leaves = sizes.shape[0]
    ends = jnp.cumsum(sizes)
    positions = offset + jnp.arange(rows_dev, dtype=jnp.int32)
    leaf_of = jnp.sum(positions[:, None] >= ends[None, :], axis=1)
    reach = rows_dev // (UNIT * MINU) + 2
    offsets = jnp.arange(reach, dtype=jnp.int32)
    levels = LEVELS + 1
    node_ids = [leaf_of // 2**level for level in range(levels)]
    totals = []
    stored_leaf = jnp.sum(placed[:, None] >= ends[None, :], axis=1)
    leaf_range = jnp.arange(leaves, dtype=jnp.int32)
    chosen = stored_leaf[None, :] == leaf_range[:, None]
    masked = jnp.where(chosen[:, :, None], sample[None, :, :], jnp.zeros((), jnp.bfloat16))
    spread = jnp.einsum("lrs,rt->lst", masked, sample, preferred_element_type=jnp.float32)
    leaf_grams = lax.psum(spread, ("row", "col"))
    for level in range(levels):
        group = 2**level
        count = leaves // group
        node_grams = leaf_grams.reshape(count, group, width, width).sum(axis=1)
        index = jnp.minimum(node_ids[level][0] + offsets, count - 1)
        totals.append(jnp.take(node_grams, index, axis=0))
    identity_matrix = jnp.eye(width, dtype=jnp.float32)
    values = tree_rows.astype(jnp.float32).T
    results = []
    for level in range(levels):
        ids = node_ids[level]
        group = 2**level
        count = leaves // group
        node_sizes = sizes.reshape(count, group).sum(axis=1)
        candidate = ids[0] + offsets
        present = candidate <= ids[-1]
        counts = jnp.take(node_sizes, jnp.minimum(candidate, count - 1)).astype(jnp.float32)
        mean = jnp.where(
            present[:, None, None], totals[level] / counts[:, None, None], identity_matrix[None]
        )
        factor = jnp.linalg.cholesky(mean)
        basis = jnp.zeros((rows_dev, width), jnp.float32)
        for which in range(reach):
            solved = jax.scipy.linalg.solve_triangular(factor[which], values, lower=True).T
            basis = basis + jnp.where((ids == candidate[which])[:, None], solved, 0.0)
        results.append(basis.astype(jnp.bfloat16))
    return jnp.stack(results)


def solution(mesh):
    return jax.shard_map(
        shards,
        mesh=mesh,
        in_specs=(P("row", "col"), P("row", None), P(), P()),
        out_specs=P(None, ("row", "col"), None),
        check_vma=False,
    )
```

profile of v0, /device:TPU:0, one launch (start us, length us, event | category | flops | bytes accessed | tf_op | source)
XLA Modules:
  0.0 1622.6 jit_solution(10285654006331508957)
XLA Ops:
  6.5 30.1 %fusion.169 = f32[4096,256]{1,0:T(8,128)} fusion(bf16[8192,4096]{1,0:T(8,128)(2,1)} %param.7, bf16[8192,256]{1,0:T(8,128)(2,1)} %param.8), kind=kOutput, calls=%fused_computation.425 | convolution fusion | flops 17179869184 | bytes 75497472 | tf_op jit(solution)/shard_map/dot_general | solution.py:13
  36.6 78.8 %all-reduce.5 = bf16[4096,256]{1,0:T(8,128)(2,1)S(1)} all-reduce(f32[4096,256]{1,0:T(8,128)} %fusion.169), channel_id=1, replica_groups=mesh['row'=4,'col'=8] {'row'}, use_global_device_ids=true, to_apply=%region_4.5 | all-reduce | flops 1048576 | bytes 6291456 | tf_op jit(solution)/shard_map/psum | solution.py:16
  115.4 30.2 %convolution_bitcast_fusion = f32[8192,256]{0,1:T(8,128)} fusion(bf16[8192,4096]{1,0:T(8,128)(2,1)} %param.7, bf16[4096,256]{1,0:T(8,128)(2,1)S(1)} %all-reduce.5), kind=kOutput, calls=%fused_computation.46 | convolution fusion | flops 17179869184 | bytes 77594624 | tf_op jit(solution)/shard_map/dot_general | solution.py:20
  146.6 120.1 %scatter_custom_fusion = s32[32768]{0:T(1024)S(1)} fusion(s32[32768]{0:T(1024)S(1)} %compare_select_fusion, s32[32768]{0:T(1024)S(1)} %iota.124, s32[]{:T(128)} %copy.190), kind=kCustom, calls=%fused_computation.279 | custom fusion | bytes 131076 | tf_op jit(solution)/shard_map/scatter | solution.py:33
  274.3 19.7 %reduce-scatter.2.cloned.1.call-done = f32[1024,256]{0,1:T(8,128)} async-done(((f32[8192,256]{0,1:T(8,128)}), f32[1024,256]{0,1:T(8,128)}) %reduce-scatter.2.cloned.1.call-update) | async-done | bytes 1048592 | tf_op jit(solution)/shard_map/reduce_scatter | solution.py:19
  359.1 131.6 %all-reduce.4.cloned.1.call-done = f32[32,256,256]{2,1,0:T(8,128)} async-done(((f32[32,256,256]{2,1,0:T(8,128)}), f32[32,256,256]{2,1,0:T(8,128)}) %all-reduce.4.cloned.1.call-update) | async-done | bytes 8388624 | tf_op jit(solution)/shard_map/psum | solution.py:62
  531.2 47.7 %custom-call.37 = f32[4,128,128]{2,1,0:T(8,128)S(1)} custom-call(f32[4,128,128]{2,1,0:T(8,128)} %cholesky.350), custom_call_target="Cholesky" | custom-call | tf_op jit(solution)/shard_map/jit(cholesky)/cholesky | solution.py:83
  584.8 48.7 %custom-call.51 = f32[4,128,128]{2,1,0:T(8,128)} custom-call(f32[4,128,128]{2,1,0:T(8,128)} %cholesky.356), custom_call_target="Cholesky" | custom-call | tf_op jit(solution)/shard_map/jit(cholesky)/cholesky | solution.py:83
  637.2 47.5 %custom-call.44 = f32[4,128,128]{2,1,0:T(8,128)} custom-call(f32[4,128,128]{2,1,0:T(8,128)S(1)} %cholesky.353), custom_call_target="Cholesky" | custom-call | tf_op jit(solution)/shard_map/jit(cholesky)/cholesky | solution.py:83
  686.3 47.1 %custom-call.58 = f32[4,128,128]{2,1,0:T(8,128)S(1)} custom-call(f32[4,128,128]{2,1,0:T(8,128)S(1)} %cholesky.359), custom_call_target="Cholesky" | custom-call | tf_op jit(solution)/shard_map/jit(cholesky)/cholesky | solution.py:83
  735.4 39.3 %custom-call.38 = f32[4,1,128,128]{2,3,1,0:T(8,128)S(1)} custom-call(f32[4,1,128,128]{3,2,1,0:T(8,128)S(1)} %get-tuple-element.324), custom_call_target="InvertDiagBlocksLowerTriangular" | custom-call | tf_op jit(solution)/shard_map/jit(cholesky)/cholesky | solution.py:83
  777.7 47.5 %custom-call.39 = f32[4,128,128]{2,1,0:T(8,128)} custom-call(f32[4,128,128]{2,1,0:T(8,128)S(1)} %convolution_subtract_fusion.19), custom_call_target="Cholesky" | custom-call | tf_op jit(solution)/shard_map/jit(cholesky)/cholesky | solution.py:83
  826.3 41.0 %custom-call.45 = f32[4,1,128,128]{2,3,1,0:T(8,128)} custom-call(f32[4,1,128,128]{3,2,1,0:T(8,128)} %get-tuple-element.322), custom_call_target="InvertDiagBlocksLowerTriangular" | custom-call | tf_op jit(solution)/shard_map/jit(cholesky)/cholesky | solution.py:83
  871.3 48.3 %custom-call.46 = f32[4,128,128]{2,1,0:T(8,128)} custom-call(f32[4,128,128]{2,1,0:T(8,128)} %convolution_subtract_fusion.18), custom_call_target="Cholesky" | custom-call | tf_op jit(solution)/shard_map/jit(cholesky)/cholesky | solution.py:83
  921.6 40.7 %custom-call.52 = f32[4,1,128,128]{2,3,1,0:T(8,128)} custom-call(f32[4,1,128,128]{3,2,1,0:T(8,128)} %get-tuple-element.321), custom_call_target="InvertDiagBlocksLowerTriangular" | custom-call | tf_op jit(solution)/shard_map/jit(cholesky)/cholesky | solution.py:83
  966.8 48.7 %custom-call.53 = f32[4,128,128]{2,1,0:T(8,128)} custom-call(f32[4,128,128]{2,1,0:T(8,128)} %convolution_subtract_fusion.17), custom_call_target="Cholesky" | custom-call | tf_op jit(solution)/shard_map/jit(cholesky)/cholesky | solution.py:83
  1016.6 40.8 %custom-call.59 = f32[4,1,128,128]{2,3,1,0:T(8,128)} custom-call(f32[4,1,128,128]{3,2,1,0:T(8,128)} %get-tuple-element.323), custom_call_target="InvertDiagBlocksLowerTriangular" | custom-call | tf_op jit(solution)/shard_map/jit(cholesky)/cholesky | solution.py:83
  1061.1 48.3 %custom-call.60 = f32[4,128,128]{2,1,0:T(8,128)} custom-call(f32[4,128,128]{2,1,0:T(8,128)} %convolution_subtract_fusion.16), custom_call_target="Cholesky" | custom-call | tf_op jit(solution)/shard_map/jit(cholesky)/cholesky | solution.py:83
  1120.3 19.8 %custom-call.64 = f32[2,128,128]{1,2,0:T(8,128)S(1)} custom-call(f32[2,128,128]{2,1,0:T(8,128)S(1)} %get-tuple-element.120), custom_call_target="InvertDiagBlocksLowerTriangular" | custom-call | tf_op jit(solution)/shard_map/jit(_solve_triangular)/triangular_solve | solution.py:86
  1200.7 19.9 %custom-call.61 = f32[2,128,128]{1,2,0:T(8,128)S(1)} custom-call(f32[2,128,128]{2,1,0:T(8,128)S(1)} %get-tuple-element.117), custom_call_target="InvertDiagBlocksLowerTriangular" | custom-call | tf_op jit(solution)/shard_map/jit(_solve_triangular)/triangular_solve | solution.py:86
  1231.7 20.5 %custom-call.57 = f32[2,128,128]{1,2,0:T(8,128)S(1)} custom-call(f32[2,128,128]{2,1,0:T(8,128)} %copy-done.47), custom_call_target="InvertDiagBlocksLowerTriangular" | custom-call | tf_op jit(solution)/shard_map/jit(_solve_triangular)/triangular_solve | solution.py:86
  1264.4 20.5 %custom-call.56 = f32[2,128,128]{1,2,0:T(8,128)S(1)} custom-call(f32[2,128,128]{2,1,0:T(8,128)} %copy-done.48), custom_call_target="InvertDiagBlocksLowerTriangular" | custom-call | tf_op jit(solution)/shard_map/jit(_solve_triangular)/triangular_solve | solution.py:86
  1297.0 20.9 %custom-call.55 = f32[2,128,128]{1,2,0:T(8,128)S(1)} custom-call(f32[2,128,128]{2,1,0:T(8,128)} %copy-done.49), custom_call_target="InvertDiagBlocksLowerTriangular" | custom-call | tf_op jit(solution)/shard_map/jit(_solve_triangular)/triangular_solve | solution.py:86
  1328.3 20.5 %custom-call.54 = f32[2,128,128]{1,2,0:T(8,128)S(1)} custom-call(f32[2,128,128]{2,1,0:T(8,128)} %copy-done.50), custom_call_target="InvertDiagBlocksLowerTriangular" | custom-call | tf_op jit(solution)/shard_map/jit(_solve_triangular)/triangular_solve | solution.py:86
  1360.6 20.5 %custom-call.50 = f32[2,128,128]{1,2,0:T(8,128)S(1)} custom-call(f32[2,128,128]{2,1,0:T(8,128)} %copy-done.51), custom_call_target="InvertDiagBlocksLowerTriangular" | custom-call | tf_op jit(solution)/shard_map/jit(_solve_triangular)/triangular_solve | solution.py:86
  1392.9 20.6 %custom-call.49 = f32[2,128,128]{1,2,0:T(8,128)S(1)} custom-call(f32[2,128,128]{2,1,0:T(8,128)} %copy-done.52), custom_call_target="InvertDiagBlocksLowerTriangular" | custom-call | tf_op jit(solution)/shard_map/jit(_solve_triangular)/triangular_solve | solution.py:86
  1425.8 20.5 %custom-call.48 = f32[2,128,128]{1,2,0:T(8,128)S(1)} custom-call(f32[2,128,128]{2,1,0:T(8,128)} %copy-done.53), custom_call_target="InvertDiagBlocksLowerTriangular" | custom-call | tf_op jit(solution)/shard_map/jit(_solve_triangular)/triangular_solve | solution.py:86
  1456.6 20.5 %custom-call.47 = f32[2,128,128]{1,2,0:T(8,128)S(1)} custom-call(f32[2,128,128]{2,1,0:T(8,128)} %copy-done.54), custom_call_target="InvertDiagBlocksLowerTriangular" | custom-call | tf_op jit(solution)/shard_map/jit(_solve_triangular)/triangular_solve | solution.py:86
  1489.4 20.7 %custom-call.43 = f32[2,128,128]{1,2,0:T(8,128)S(1)} custom-call(f32[2,128,128]{2,1,0:T(8,128)} %copy-done.55), custom_call_target="InvertDiagBlocksLowerTriangular" | custom-call | tf_op jit(solution)/shard_map/jit(_solve_triangular)/triangular_solve | solution.py:86
  1522.2 20.5 %custom-call.42 = f32[2,128,128]{1,2,0:T(8,128)S(1)} custom-call(f32[2,128,128]{2,1,0:T(8,128)} %copy-done.56), custom_call_target="InvertDiagBlocksLowerTriangular" | custom-call | tf_op jit(solution)/shard_map/jit(_solve_triangular)/triangular_solve | solution.py:86
  1554.4 20.5 %custom-call.41 = f32[2,128,128]{1,2,0:T(8,128)S(1)} custom-call(f32[2,128,128]{2,1,0:T(8,128)} %copy-done.57), custom_call_target="InvertDiagBlocksLowerTriangular" | custom-call | tf_op jit(solution)/shard_map/jit(_solve_triangular)/triangular_solve | solution.py:86
  1585.3 20.7 %custom-call.40 = f32[2,128,128]{1,2,0:T(8,128)S(1)} custom-call(f32[2,128,128]{2,1,0:T(8,128)} %copy-done.46), custom_call_target="InvertDiagBlocksLowerTriangular" | custom-call | tf_op jit(solution)/shard_map/jit(_solve_triangular)/triangular_solve | solution.py:86
  (458 shorter events, 459.0 us)
Async XLA Ops:
  6.5 287.5 %reduce-scatter.2.cloned.1.call-start = ((), (), s32[]{:S(2)}) async-start(), calls=%async_computation.2 | async-start | bytes 9437184 | tf_op jit(solution)/shard_map/reduce_scatter | solution.py:19
  145.6 345.1 %all-reduce.4.cloned.1.call-start = ((), (), s32[]{:S(2)}) async-start(), calls=%async_computation.3 | async-start | bytes 16777216 | tf_op jit(solution)/shard_map/psum | solution.py:62
  329.1 25.8 %all-to-all-start = ((bf16[32,32,256]{2,1,0:T(8,128)(2,1)}), bf16[32,32,256]{2,1,0:T(8,128)(2,1)S(1)}, u32[]{:S(2)}, u32[]{:S(2)}) async-start(bf16[32,32,256]{2,1,0:T(8,128)(2,1)} %bitcast.13), calls=%async_computation.1 | async-start | bytes 1048576 | tf_op jit(solution)/shard_map/all_to_all | solution.py:41
  513.8 7.3 copy-start.66
  513.8 7.3 copy-start.67
  514.4 6.7 copy-start.68
  733.3 44.4 %copy-start.30 = (f32[4,128,128]{2,1,0:T(8,128)}, f32[4,128,128]{2,1,0:T(8,128)S(1)}, u32[]{:S(2)}) copy-start(f32[4,128,128]{2,1,0:T(8,128)S(1)} %custom-call.58) | copy-start | bytes 786436
  868.7 98.1 %copy-start.25 = (f32[4,256,256]{2,1,0:T(8,128)}, f32[4,256,256]{2,1,0:T(8,128)S(1)}, u32[]{:S(2)}) copy-start(f32[4,256,256]{2,1,0:T(8,128)S(1)} %get-tuple-element.372) | copy-start | bytes 3145732
  1112.9 3.6 copy-start.71
  1220.5 2.7 copy-start.24
  1348.8 3.5 copy-start.23
  1477.1 3.5 copy-start.22
  1606.0 3.9 copy-start.1
  1606.0 3.9 copy-start.3
  1606.1 3.9 copy-start.5
  1606.1 3.9 copy-start.7
  1606.1 3.9 copy-start.34
  1606.1 3.9 copy-start.35
  1606.1 3.9 copy-start.36
  1606.1 3.9 copy-start.37
  1606.1 3.9 copy-start.62
  1606.1 3.9 copy-start.63
  1606.1 3.9 copy-start.64
  1606.1 3.9 copy-start.65
  1608.1 2.6 copy-start.9
  1608.1 2.6 copy-start.11
  1608.1 2.6 copy-start.13
  1608.1 2.6 copy-start.15
  1608.1 2.6 copy-start.38
  1608.1 2.6 copy-start.39
  1608.1 2.6 copy-start.40
  1608.1 2.6 copy-start.41
  (43 other events, 48.4 us)
Sparse Core Ops, SparseCore 0:
  145.7 148.2 reduce-scatter.1
  302.2 188.4 all-reduce.3
where the time goes:
time: 1630 us; the launch traced here: 1620 us
  other arithmetic  944 us (58%)
  local copies, waits for them, and re-layouts  286 us (18%)
  waiting for transfers between devices  162 us (10%)
  matrix products  131 us (8%)
  blocking collectives  78.8 us (5%)
    another operation x28, other arithmetic, shards(): factor = jnp.linalg.cholesky(mean)  551 us
    another operation x22, other arithmetic, shards(): jax.scipy.linalg.solve_triangular(factor[which], values, lower=True)  329 us
    psum x1, waiting for transfers between devices, shards(): leaf_grams = lax.psum(spread, ('row', 'col'))  132 us
    scatter x1, local copies, waits for them, and re-layouts, shards(): inverse = jnp.zeros((total_rows,), jnp.int32).at[tree_perm].set(jnp.arang...  120 us
    another operation x113, local copies, waits for them, and re-layouts, shards(): jax.scipy.linalg.solve_triangular(factor[which], values, lower=True)  95 us
    psum x1, blocking collectives, shards(): sample_w = lax.psum(partial_w, 'row').astype(jnp.bfloat16)  78.8 us
    another operation x48, matrix products, shards(): jax.scipy.linalg.solve_triangular(factor[which], values, lower=True)  49.2 us
  transfers between devices with their start and end apart: 3, of which 3 were waited for; matrix products, arithmetic and copies ran while one was open for 10% of the time, Pallas kernels for 0%

commit v1 on v0

v1 whole, which is shorter than its diff:
```python
import functools

import jax
import jax.numpy as jnp
from jax import lax
from jax.experimental import pallas as pl
from jax.experimental.pallas import tpu as pltpu
from jax.sharding import PartitionSpec as P

UNIT = 128
MINU = 4
MOSTU = 8
LEVELS = 3
BLOCK = 64
HIGHEST = lax.Precision.HIGHEST


def basis_kernel(index_ref, gram_ref, rows_ref, out_ref, work, block, high, low):
    nodes, width, _ = gram_ref.shape
    count = width // BLOCK
    eye = (
        lax.broadcasted_iota(jnp.int32, (width, width), 0)
        == lax.broadcasted_iota(jnp.int32, (width, width), 1)
    ).astype(jnp.float32)

    @pl.loop(0, nodes)
    def _(node):
        work[node, :, :width] = gram_ref[node]
        work[node, :, width:] = eye

    small = (
        lax.broadcasted_iota(jnp.int32, (nodes, BLOCK, BLOCK), 1)
        == lax.broadcasted_iota(jnp.int32, (nodes, BLOCK, BLOCK), 2)
    )

    @pl.loop(0, count)
    def _(step):
        for which in range(count):

            @pl.when(step == which)
            def _():
                start = which * BLOCK
                block[:, :, :BLOCK] = work[:, start : start + BLOCK, start : start + BLOCK]
                block[:, :, BLOCK:] = small.astype(jnp.float32)

        for column in range(BLOCK - 1):
            base = column // 8 * 8
            rest = block[:, base:, :]
            pivot_row = rest[:, column - base : column - base + 1, :]
            scale = 1.0 / pivot_row[:, :, column : column + 1]
            below = (
                lax.broadcasted_iota(jnp.int32, (nodes, BLOCK - base, 1), 1) > column - base
            )
            factor = jnp.where(below, rest[:, :, column : column + 1], 0.0)
            block[:, base:, :] = rest - factor * (pivot_row * scale)
        pivots = jnp.sum(jnp.where(small, block[:, :, :BLOCK], 0.0), axis=2, keepdims=True)
        block[:, :, BLOCK:] = block[:, :, BLOCK:] * lax.rsqrt(pivots)

        for which in range(count):

            @pl.when(step == which)
            def _():
                start = which * BLOCK
                after = start + BLOCK
                left = start // 128 * 128
                right = width + (after + 127) // 128 * 128

                @pl.loop(0, nodes)
                def _(node):
                    inverse = block[node][:, BLOCK:]
                    solved = jnp.dot(
                        inverse,
                        work[node, start:after, left:right],
                        preferred_element_type=jnp.float32,
                        precision=HIGHEST,
                    )
                    work[node, start:after, left:right] = solved
                    if after < width:
                        panel = solved[:, : width - left].T
                        change = jnp.dot(
                            panel[after - left :, :],
                            solved,
                            preferred_element_type=jnp.float32,
                            precision=HIGHEST,
                        )
                        work[node, after:, left:right] = work[node, after:, left:right] - change

    @pl.loop(0, nodes)
    def _(node):
        full = work[node, :, width:]
        top = full.astype(jnp.bfloat16)
        high[node] = top
        low[node] = (full - top.astype(jnp.float32)).astype(jnp.bfloat16)

    levels, rows, _ = out_ref.shape
    units = rows // UNIT

    @pl.loop(0, levels)
    def _(level):
        @pl.loop(0, units)
        def _(unit):
            node = index_ref[level * units + unit]
            where = pl.ds(pl.multiple_of(unit * UNIT, UNIT), UNIT)
            values = rows_ref[where, :]
            contract = (((1,), (1,)), ((), ()))
            total = lax.dot_general(
                values, low[node], contract, preferred_element_type=jnp.float32
            ) + lax.dot_general(values, high[node], contract, preferred_element_type=jnp.float32)
            out_ref[level, where, :] = total.astype(jnp.bfloat16)


def make_bases(index, grams, rows, levels):
    nodes, width, _ = grams.shape
    return pl.pallas_call(
        basis_kernel,
        out_shape=jax.ShapeDtypeStruct((levels, rows.shape[0], width), jnp.bfloat16),
        in_specs=[
            pl.BlockSpec(memory_space=pltpu.SMEM),
            pl.BlockSpec(memory_space=pltpu.VMEM),
            pl.BlockSpec(memory_space=pltpu.VMEM),
        ],
        out_specs=pl.BlockSpec(memory_space=pltpu.VMEM),
        scratch_shapes=[
            pltpu.VMEM((nodes, width, 2 * width), jnp.float32),
            pltpu.VMEM((nodes, BLOCK, 2 * BLOCK), jnp.float32),
            pltpu.VMEM((nodes, width, width), jnp.bfloat16),
            pltpu.VMEM((nodes, width, width), jnp.bfloat16),
        ],
        compiler_params=pltpu.CompilerParams(vmem_limit_bytes=40 * 2**20),
    )(index, grams, rows)


def to_tree_order(sample, tree_perm):
    rows_dev, width = sample.shape
    devices = tree_perm.shape[0] // rows_dev
    device = lax.axis_index(("row", "col"))
    capacity = (rows_dev + devices - 1) // devices
    grid = tree_perm.reshape(devices, rows_dev)
    mine = grid // rows_dev == device
    rank = jnp.cumsum(mine.astype(jnp.int32), axis=1) - 1
    slots = jnp.arange(capacity, dtype=jnp.int32)
    chosen = mine[:, None, :] & (rank[:, None, :] == slots[None, :, None])
    send = jnp.sum(jnp.where(chosen, (grid % rows_dev)[:, None, :], 0), axis=2).reshape(-1)
    outgoing = jnp.take(sample, send, axis=0, mode="clip")
    incoming = lax.all_to_all(outgoing, ("row", "col"), split_axis=0, concat_axis=0, tiled=True)
    wanted = lax.dynamic_slice_in_dim(tree_perm, device * rows_dev, rows_dev)
    source = wanted // rows_dev
    order = jnp.arange(rows_dev, dtype=jnp.int32)
    ahead = (source[None, :] == source[:, None]) & (order[None, :] < order[:, None])
    pick = source * capacity + jnp.sum(ahead, axis=1)
    return jnp.take(incoming, pick, axis=0, mode="clip")


def bases_of(sample, tree_perm, leaf_units):
    rows_dev, width = sample.shape
    devices = tree_perm.shape[0] // rows_dev
    device = lax.axis_index(("row", "col"))
    tree_rows = to_tree_order(sample, tree_perm)
    sizes = UNIT * (MINU - 1 + leaf_units)
    leaves = sizes.shape[0]
    ends = jnp.cumsum(sizes)
    levels = LEVELS + 1
    units = rows_dev // UNIT
    starts = jnp.arange(devices, dtype=jnp.int32) * rows_dev
    first_leaf = jnp.sum(starts[:, None] >= ends[None, :], axis=1)
    last_leaf = jnp.sum((starts + rows_dev - 1)[:, None] >= ends[None, :], axis=1)
    unit_start = device * rows_dev + jnp.arange(units, dtype=jnp.int32) * UNIT
    unit_leaf = jnp.sum(unit_start[:, None] >= ends[None, :], axis=1)

    reach = [2 + max(rows_dev - 2 * UNIT, 0) // (UNIT * MINU * 2**t) for t in range(levels)]
    first = jnp.take(first_leaf, device)
    touched = first + jnp.arange(reach[0], dtype=jnp.int32)
    unit_mask = (unit_leaf[None, :] == touched[:, None]).astype(jnp.bfloat16)
    mask = jnp.repeat(unit_mask, UNIT, axis=1)
    partial = jnp.stack(
        [
            lax.dot_general(
                tree_rows * mask[which][:, None],
                tree_rows,
                (((0,), (0,)), ((), ())),
                preferred_element_type=jnp.float32,
            )
            for which in range(reach[0])
        ]
    )

    def pick_nodes(level, nodes):
        chosen = touched // 2**level == nodes
        return jnp.sum(jnp.where(chosen[:, None, None], partial, 0.0), axis=0)

    wanted = []
    local = LEVELS - 1
    for level in range(local):
        group = 2**level
        low, high = first_leaf // group, last_leaf // group
        my_low, my_high = jnp.take(low, device), jnp.take(high, device)
        span = (UNIT * (MINU - 1 + MOSTU) * group - 2 * UNIT) // rows_dev + 1
        head, tail = pick_nodes(level, my_low), pick_nodes(level, my_high)
        to_head = jnp.zeros_like(head)
        to_tail = jnp.zeros_like(head)
        for shift in range(1, span + 1):
            up = lax.ppermute(
                tail, ("row", "col"), [(i, i + shift) for i in range(devices - shift)]
            )
            down = lax.ppermute(
                head, ("row", "col"), [(i + shift, i) for i in range(devices - shift)]
            )
            before = jnp.take(high, jnp.maximum(device - shift, 0))
            behind = jnp.take(low, jnp.minimum(device + shift, devices - 1))
            use_up = (device >= shift) & (before == my_low)
            use_down = (device + shift < devices) & (behind == my_high)
            to_head = to_head + jnp.where(use_up, up, 0.0)
            to_tail = to_tail + jnp.where(use_down, down, 0.0)
        for which in range(reach[level]):
            node = my_low + which
            gram = pick_nodes(level, node)
            gram = gram + jnp.where(node == my_low, to_head, 0.0)
            wanted.append(gram + jnp.where(node == my_high, to_tail, 0.0))
    group = 2**local
    count = leaves // group
    spread = jnp.stack([pick_nodes(local, node) for node in range(count)])
    shared = lax.psum(spread, ("row", "col"))
    for level in range(local, levels):
        grams = shared.reshape(leaves // 2**level, 2 ** (level - local), width, width).sum(axis=1)
        index = first // 2**level + jnp.arange(reach[level], dtype=jnp.int32)
        taken = jnp.take(grams, jnp.minimum(index, leaves // 2**level - 1), axis=0)
        wanted.extend(taken[which] for which in range(reach[level]))

    slot = 0
    last = jnp.take(last_leaf, device)
    eye = jnp.eye(width, dtype=jnp.float32)
    index = []
    for level in range(levels):
        group = 2**level
        node_sizes = sizes.reshape(leaves // group, group).sum(axis=1)
        low, high = first // group, last // group
        for which in range(reach[level]):
            node = low + which
            rows = jnp.take(node_sizes, jnp.minimum(node, leaves // group - 1))
            mean = wanted[slot + which] / rows.astype(jnp.float32)
            wanted[slot + which] = jnp.where(node <= high, mean, eye)
        index.append(slot + unit_leaf // group - low)
        slot += reach[level]
    return make_bases(jnp.concatenate(index), jnp.stack(wanted), tree_rows, levels)


def shards(kernel, random_cols, tree_perm, leaf_units):
    width = random_cols.shape[1]
    parts = lax.axis_size("row")
    partial_w = lax.dot_general(
        kernel, random_cols, (((0,), (0,)), ((), ())), preferred_element_type=jnp.float32
    ).astype(jnp.bfloat16)
    pieces = lax.all_to_all(partial_w, "row", split_axis=0, concat_axis=0, tiled=True)
    piece = jnp.sum(pieces.reshape(parts, -1, width).astype(jnp.float32), axis=0)
    sample_w = lax.all_gather(piece.astype(jnp.bfloat16), "row", axis=0, tiled=True)
    columns = lax.axis_size("col")
    partial = jnp.dot(kernel, sample_w, preferred_element_type=jnp.float32).astype(jnp.bfloat16)
    pieces = lax.all_to_all(partial, "col", split_axis=0, concat_axis=0, tiled=True)
    sample = jnp.sum(pieces.reshape(columns, -1, width).astype(jnp.float32), axis=0)
    return bases_of(sample.astype(jnp.bfloat16), tree_perm, leaf_units)


def solution(mesh):
    return jax.shard_map(
        shards,
        mesh=mesh,
        in_specs=(P("row", "col"), P("row", None), P(), P()),
        out_specs=P(None, ("row", "col"), None),
        check_vma=False,
    )
```

time: 1630 us -> 512 us (0.31)
  other arithmetic: 944 us -> 30 us
  local copies, waits for them, and re-layouts: 286 us -> 25.1 us
  waiting for transfers between devices: 162 us -> 241 us
  matrix products: 131 us -> 60 us
  Pallas kernels: 0 us -> 60 us
  blocking collectives: 78.8 us -> 29.9 us
  starting transfers between devices: 4.14 us -> 35.9 us
    another operation x57 -> x5, other arithmetic: 884 us -> 9.25 us  [the longest x28 551 us: shards(): factor = jnp.linalg.cholesky(mean)]
    scatter x2 -> x0, local copies, waits for them, and re-layouts: 126 us -> none  [the longest x1 120 us: shards(): inverse = jnp.zeros((total_rows,), jnp.int32).at[tree_perm].set(jnp.arang...]
    another operation x123 -> x10, local copies, waits for them, and re-layouts: 103 us -> 4.24 us  [the longest x4 2.68 us: bases_of(): rows = jnp.take(node_sizes, jnp.minimum(node, leaves // group - 1))]
    psum x1 -> x0, blocking collectives: 78.8 us -> none  [shards(): sample_w = lax.psum(partial_w, 'row').astype(jnp.bfloat16)]
    all_to_all x1 -> x2, waiting for transfers between devices: 10.5 us -> 77.4 us  [the longest x1 76.7 us: shards(): lax.all_to_all(partial, 'col', split_axis=0, concat_axis=0, tiled=True)]
    another operation x56 -> x0, matrix products: 64.4 us -> none  [the longest x48 49.2 us: shards(): jax.scipy.linalg.solve_triangular(factor[which], values, lower=True)]
    pallas_call x0 -> x1, Pallas kernels: none -> 60 us  [make_bases(): pl.pallas_call(basis_kernel, out_shape=jax.ShapeDtypeStruct((levels, rows...]
    all_to_all x0 -> x1, blocking collectives: none -> 29.9 us  [shards(): lax.all_to_all(partial_w, 'row', split_axis=0, concat_axis=0, tiled=True)]
  transfers between devices with their start and end apart: 3 -> 14, of which waited for: 3 -> 7; matrix products, arithmetic and copies ran while one was open for 10% -> 4% of each run, Pallas kernels for 0% -> 0%
where the time goes in v1:
time: 512 us; the launch traced here: 511 us
  waiting for transfers between devices  241 us (47%)
  matrix products  60 us (12%)
  Pallas kernels  60 us (12%)
  starting transfers between devices  35.9 us (7%)
  other arithmetic  30 us (6%)
  blocking collectives  29.9 us (6%)
  between operations  28.7 us (6%)
  local copies, waits for them, and re-layouts  25.1 us (5%)
    psum x1, waiting for transfers between devices, bases_of(): shared = lax.psum(spread, ('row', 'col'))  115 us
    all_to_all x1, waiting for transfers between devices, shards(): lax.all_to_all(partial, 'col', split_axis=0, concat_axis=0, tiled=True)  76.7 us
    pallas_call x1, Pallas kernels, make_bases(): pl.pallas_call(basis_kernel, out_shape=jax.ShapeDtypeStruct((levels, rows...  60 us
    all_to_all x1, blocking collectives, shards(): lax.all_to_all(partial_w, 'row', split_axis=0, concat_axis=0, tiled=True)  29.9 us
    dot_general x1, matrix products, shards(): lax.dot_general(kernel, random_cols, (((0,), (0,)), ((), ())), preferred_...  29.5 us
    dot_general x1, matrix products, shards(): jnp.dot(kernel, sample_w, preferred_element_type=jnp.float32)  28.9 us
    all_gather x1, waiting for transfers between devices, shards(): lax.all_gather(piece.astype(jnp.bfloat16), 'row', axis=0, tiled=True)  23.8 us
    ppermute x5, starting transfers between devices, bases_of(): lax.ppermute(tail, ('row', 'col'), [(i, i + shift) for i in range(devices...  20.8 us
  transfers between devices with their start and end apart: 14, of which 7 were waited for; matrix products, arithmetic and copies ran while one was open for 4% of the time, Pallas kernels for 0%

profile of v1, /device:TPU:0, one launch (start us, length us, event | category | flops | bytes accessed | tf_op | source)
XLA Modules:
  0.0 510.9 jit_solution(17689572395124004348)
XLA Ops:
  6.5 29.5 %convolution_convert_fusion.1 = bf16[4096,256]{1,0:T(8,128)(2,1)} fusion(bf16[8192,4096]{1,0:T(8,128)(2,1)} %param.4, bf16[8192,256]{1,0:T(8,128)(2,1)} %param.5), kind=kOutput, calls=%fused_computation.5 | convolution fusion | flops 17180917760 | bytes 73400320 | tf_op jit(solution)/shard_map/dot_general | solution.py:250
  36.0 29.9 %all_to_all.30 = bf16[4,1024,256]{2,1,0:T(8,128)(2,1)S(1)} all-to-all(bf16[4,1024,256]{2,1,0:T(8,128)(2,1)} %bitcast.142), channel_id=1, replica_groups=mesh['row'=4,'col'=8] {'row'}, dimensions={0} | all-to-all | bytes 4194304 | tf_op jit(solution)/shard_map/all_to_all | solution.py:253
  67.2 23.8 %all-gather.2.cloned.1.call-done = bf16[4096,256]{1,0:T(8,128)(2,1)} async-done(((bf16[1024,256]{1,0:T(8,128)(2,1)}), bf16[4096,256]{1,0:T(8,128)(2,1)}) %all-gather.2.cloned.1.call-update) | async-done | bytes 2097168 | tf_op jit(solution)/shard_map/all_gather | solution.py:255
  91.0 28.9 %convolution_convert_fusion = bf16[256,8192]{1,0:T(8,128)(2,1)} fusion(bf16[4096,256]{1,0:T(8,128)(2,1)} %all-gather.2.cloned.1.call-done, bf16[8192,4096]{1,0:T(8,128)(2,1)} %param.4), kind=kOutput, calls=%fused_computation.4 | convolution fusion | flops 17181966336 | bytes 73400320 | tf_op jit(solution)/shard_map/dot_general | solution.py:257
  119.9 4.7 copy.26
  124.7 5.6 %all-to-all-start.1 = ((bf16[8,1024,256]{1,2,0:T(8,128)(2,1)}), bf16[8,1024,256]{1,2,0:T(8,128)(2,1)}, u32[]{:S(2)}, u32[]{:S(2)}) async-start(bf16[8,1024,256]{1,2,0:T(8,128)(2,1)} %bitcast.140), calls=%async_computation.1 | async-start | bytes 8388608 | tf_op jit(solution)/shard_map/all_to_all | solution.py:258
  135.1 9.0 %reduce-window.19 = s32[32,8,128]{2,1,0:T(8,128)S(1)} reduce-window(s32[32,8,128]{2,1,0:T(8,128)S(1)} %fusion.28, s32[]{:T(128)} %constant.471.clone.1), window={size=1x1x128 pad=0_0x0_0x127_0}, to_apply=%region_6.7 | reduce-window | flops 4161536 | bytes 262148 | tf_op jit(solution)/shard_map/reduce-window.1
  147.3 76.7 %all-to-all-done.1 = bf16[8,1024,256]{1,2,0:T(8,128)(2,1)} async-done(((bf16[8,1024,256]{1,2,0:T(8,128)(2,1)}), bf16[8,1024,256]{1,2,0:T(8,128)(2,1)}, u32[]{:S(2)}, u32[]{:S(2)}) %all-to-all-start.1) | async-done | bytes 4194336 | tf_op jit(solution)/shard_map/all_to_all | solution.py:258
  224.0 3.1 reduce_sum.260
  227.3 5.0 gather_fusion
  232.3 2.7 all-to-all-start.2
  251.3 3.9 gather_fusion.1
  256.8 1.4 select_reduce_fusion.1
  258.2 2.9 collective-permute-start.1
  261.1 4.1 collective-permute-start
  265.2 1.3 collective-permute-start.3
  266.5 1.3 collective-permute-start.2
  267.8 1.5 select_reduce_fusion.3
  269.3 7.3 %collective-permute-start.6 = (f32[256,256]{1,0:T(8,128)}, f32[256,256]{1,0:T(8,128)}, u32[]{:S(2)}, u32[]{:S(2)}) collective-permute-start(f32[256,256]{1,0:T(8,128)} %get-tuple-element.282), channel_id=1, source_target_pairs={{0,3},{1,4},{2,5},{3,6},{4,7},{5,8},{6,9},{7,10},{8,11},{9,12},{10... | collective-permute-start | bytes 786440 | tf_op jit(solution)/shard_map/ppermute | solution.py:202
  276.8 1.3 copy-done
  278.2 2.8 collective-permute-start.5
  281.1 3.6 collective-permute-start.4
  284.7 1.3 collective-permute-start.9
  286.0 1.3 collective-permute-start.8
  288.5 1.5 collective-permute-start.7
  291.2 3.6 collective-permute-done.5
  295.6 20.7 %collective-permute-done.9 = f32[256,256]{1,0:T(8,128)S(1)} collective-permute-done((f32[256,256]{1,0:T(8,128)}, f32[256,256]{1,0:T(8,128)S(1)}, u32[]{:S(2)}, u32[]{:S(2)}) %collective-permute-start.9) | collective-permute-done | bytes 262176 | tf_op jit(solution)/shard_map/ppermute | solution.py:205
  317.5 114.9 %all-reduce.2.cloned.1.call-done = f32[8,256,256]{2,1,0:T(8,128)} async-done(((f32[8,256,256]{2,1,0:T(8,128)}), f32[8,256,256]{2,1,0:T(8,128)}) %all-reduce.2.cloned.1.call-update) | async-done | bytes 2097168 | tf_op jit(solution)/shard_map/psum | solution.py:222
  432.3 2.2 gather_fusion.2
  435.4 2.8 bitcast_reduce_fusion
  438.3 2.6 gather_fusion.3
  444.1 60.0 %shard_map.46 = bf16[4,1024,256]{2,1,0:T(8,128)(2,1)} custom-call(s32[32]{0:T(128)S(1)} %pad_add_fusion.index_ref, f32[9,256,256]{2,1,0:T(8,128)S(1)} %fusion.8.gram_ref, bf16[1024,256]{1,0:T(8,128)(2,1)S(1)} %gather_fusion.1), custom_call_target="tpu_custom_call" | custom-call | tf_op jit(solution)/shard_map/pallas_call | solution.py:114
  (119 shorter events, 20.9 us)
Async XLA Ops:
  6.5 84.5 %all-gather.2.cloned.1.call-start = ((), (), s32[]{:S(2)}) async-start(), calls=%async_computation.3 | async-start | bytes 2621440 | tf_op jit(solution)/shard_map/all_gather | solution.py:255
  124.7 5.7 %copy-start.6 = (s32[32]{0:T(128)S(1)}, s32[32]{0:T(128)}, u32[]{:S(2)}) copy-start(s32[32]{0:T(128)} %param.7) | copy-start | bytes 388
  124.7 10.3 %copy-start.4 = (s32[32768]{0:T(1024)S(1)}, s32[32768]{0:T(1024)}, u32[]{:S(2)}) copy-start(s32[32768]{0:T(1024)} %param.6) | copy-start | bytes 393220
  124.7 99.3 %all-to-all-start.1 = ((bf16[8,1024,256]{1,2,0:T(8,128)(2,1)}), bf16[8,1024,256]{1,2,0:T(8,128)(2,1)}, u32[]{:S(2)}, u32[]{:S(2)}) async-start(bf16[8,1024,256]{1,2,0:T(8,128)(2,1)} %bitcast.140), calls=%async_computation.1 | async-start | bytes 8388608 | tf_op jit(solution)/shard_map/all_to_all | solution.py:258
  232.3 19.0 %all-to-all-start.2 = ((bf16[32,32,256]{2,1,0:T(8,128)(2,1)}), bf16[32,32,256]{2,1,0:T(8,128)(2,1)S(1)}, u32[]{:S(2)}, u32[]{:S(2)}) async-start(bf16[32,32,256]{2,1,0:T(8,128)(2,1)} %bitcast.8), calls=%async_computation.2 | async-start | bytes 1048576 | tf_op jit(solution)/shard_map/all_to_all | solution.py:145
  235.0 197.3 %all-reduce.2.cloned.1.call-start = ((), (), s32[]{:S(2)}) async-start(), calls=%async_computation.4 | async-start | bytes 4194304 | tf_op jit(solution)/shard_map/psum | solution.py:222
  258.2 18.5 %copy-start.1 = (f32[256,256]{1,0:T(8,128)}, f32[256,256]{1,0:T(8,128)S(1)}, u32[]{:S(2)}) copy-start(f32[256,256]{1,0:T(8,128)S(1)} %get-tuple-element.285) | copy-start | bytes 786436
  258.2 20.0 %collective-permute-start.1 = (f32[256,256]{1,0:T(8,128)}, f32[256,256]{1,0:T(8,128)S(1)}, u32[]{:S(2)}, u32[]{:S(2)}) collective-permute-start(f32[256,256]{1,0:T(8,128)} %get-tuple-element.259), channel_id=1, source_target_pairs={{0,2},{1,3},{2,4},{3,5},{4,6},{5,7},{6,8},{7,9},{8,10},{9,11},{10,... | collective-permute-start | bytes 786440 | tf_op jit(solution)/shard_map/ppermute | solution.py:202
  261.1 19.9 %collective-permute-start = (f32[256,256]{1,0:T(8,128)}, f32[256,256]{1,0:T(8,128)}, u32[]{:S(2)}, u32[]{:S(2)}) collective-permute-start(f32[256,256]{1,0:T(8,128)} %get-tuple-element.259), channel_id=1, source_target_pairs={{0,1},{1,2},{2,3},{3,4},{4,5},{5,6},{6,7},{7,8},{8,9},{9,10},{10,1... | collective-permute-start | bytes 786440 | tf_op jit(solution)/shard_map/ppermute | solution.py:202
  265.2 19.5 %collective-permute-start.3 = (f32[256,256]{1,0:T(8,128)S(1)}, f32[256,256]{1,0:T(8,128)}, u32[]{:S(2)}, u32[]{:S(2)}) collective-permute-start(f32[256,256]{1,0:T(8,128)S(1)} %get-tuple-element.285), channel_id=1, source_target_pairs={{2,0},{3,1},{4,2},{5,3},{6,4},{7,5},{8,6},{9,7},{10,8},{11,9},{12,... | collective-permute-start | bytes 786440 | tf_op jit(solution)/shard_map/ppermute | solution.py:205
  266.5 19.5 %collective-permute-start.2 = (f32[256,256]{1,0:T(8,128)S(1)}, f32[256,256]{1,0:T(8,128)}, u32[]{:S(2)}, u32[]{:S(2)}) collective-permute-start(f32[256,256]{1,0:T(8,128)S(1)} %get-tuple-element.285), channel_id=1, source_target_pairs={{1,0},{2,1},{3,2},{4,3},{5,4},{6,5},{7,6},{8,7},{9,8},{10,9},{11,1... | collective-permute-start | bytes 786440 | tf_op jit(solution)/shard_map/ppermute | solution.py:205
  269.3 19.2 %collective-permute-start.6 = (f32[256,256]{1,0:T(8,128)}, f32[256,256]{1,0:T(8,128)}, u32[]{:S(2)}, u32[]{:S(2)}) collective-permute-start(f32[256,256]{1,0:T(8,128)} %get-tuple-element.282), channel_id=1, source_target_pairs={{0,3},{1,4},{2,5},{3,6},{4,7},{5,8},{6,9},{7,10},{8,11},{9,12},{10... | collective-permute-start | bytes 786440 | tf_op jit(solution)/shard_map/ppermute | solution.py:202
  276.8 1.3 copy-start
  278.2 12.9 %copy-start.2 = (f32[256,256]{1,0:T(8,128)S(1)}, f32[256,256]{1,0:T(8,128)}, u32[]{:S(2)}) copy-start(f32[256,256]{1,0:T(8,128)} %get-tuple-element.261) | copy-start | bytes 786436
  278.2 9.1 %copy-start.5 = (f32[256,256]{1,0:T(8,128)}, f32[256,256]{1,0:T(8,128)S(1)}, u32[]{:S(2)}) copy-start(f32[256,256]{1,0:T(8,128)S(1)} %collective-permute-done.1) | copy-start | bytes 786436
  278.2 16.6 %collective-permute-start.5 = (f32[256,256]{1,0:T(8,128)}, f32[256,256]{1,0:T(8,128)S(1)}, u32[]{:S(2)}, u32[]{:S(2)}) collective-permute-start(f32[256,256]{1,0:T(8,128)} %get-tuple-element.282), channel_id=1, source_target_pairs={{0,2},{1,3},{2,4},{3,5},{4,6},{5,7},{6,8},{7,9},{8,10},{9,11},{10,... | collective-permute-start | bytes 786440 | tf_op jit(solution)/shard_map/ppermute | solution.py:202
  281.1 14.5 %collective-permute-start.4 = (f32[256,256]{1,0:T(8,128)}, f32[256,256]{1,0:T(8,128)S(1)}, u32[]{:S(2)}, u32[]{:S(2)}) collective-permute-start(f32[256,256]{1,0:T(8,128)} %get-tuple-element.282), channel_id=1, source_target_pairs={{0,1},{1,2},{2,3},{3,4},{4,5},{5,6},{6,7},{7,8},{8,9},{9,10},{10,1... | collective-permute-start | bytes 786440 | tf_op jit(solution)/shard_map/ppermute | solution.py:202
  284.7 31.6 %collective-permute-start.9 = (f32[256,256]{1,0:T(8,128)}, f32[256,256]{1,0:T(8,128)S(1)}, u32[]{:S(2)}, u32[]{:S(2)}) collective-permute-start(f32[256,256]{1,0:T(8,128)} %get-tuple-element.283), channel_id=1, source_target_pairs={{3,0},{4,1},{5,2},{6,3},{7,4},{8,5},{9,6},{10,7},{11,8},{12,9},{13... | collective-permute-start | bytes 786440 | tf_op jit(solution)/shard_map/ppermute | solution.py:205
  286.0 30.3 %collective-permute-start.8 = (f32[256,256]{1,0:T(8,128)}, f32[256,256]{1,0:T(8,128)S(1)}, u32[]{:S(2)}, u32[]{:S(2)}) collective-permute-start(f32[256,256]{1,0:T(8,128)} %get-tuple-element.283), channel_id=1, source_target_pairs={{2,0},{3,1},{4,2},{5,3},{6,4},{7,5},{8,6},{9,7},{10,8},{11,9},{12,... | collective-permute-start | bytes 786440 | tf_op jit(solution)/shard_map/ppermute | solution.py:205
  288.5 27.8 %collective-permute-start.7 = (f32[256,256]{1,0:T(8,128)}, f32[256,256]{1,0:T(8,128)S(1)}, u32[]{:S(2)}, u32[]{:S(2)}) collective-permute-start(f32[256,256]{1,0:T(8,128)} %get-tuple-element.283), channel_id=1, source_target_pairs={{1,0},{2,1},{3,2},{4,3},{5,4},{6,5},{7,6},{8,7},{9,8},{10,9},{11,1... | collective-permute-start | bytes 786440 | tf_op jit(solution)/shard_map/ppermute | solution.py:205
  290.0 27.4 %copy-start.3 = (f32[256,256]{1,0:T(8,128)S(1)}, f32[256,256]{1,0:T(8,128)}, u32[]{:S(2)}) copy-start(f32[256,256]{1,0:T(8,128)} %get-tuple-element.281) | copy-start | bytes 786436
Sparse Core Ops, SparseCore 0:
  67.3 23.6 all-gather.1
  278.3 154.0 all-reduce.1

commit v2 on v1

--- a/solution.py
+++ b/solution.py
@@ -1,5 +1,3 @@
-import functools
-
 import jax
 import jax.numpy as jnp
 from jax import lax
@@ -168,63 +166,69 @@
     unit_leaf = jnp.sum(unit_start[:, None] >= ends[None, :], axis=1)
 
     reach = [2 + max(rows_dev - 2 * UNIT, 0) // (UNIT * MINU * 2**t) for t in range(levels)]
+    half = width // 2
     first = jnp.take(first_leaf, device)
     touched = first + jnp.arange(reach[0], dtype=jnp.int32)
     unit_mask = (unit_leaf[None, :] == touched[:, None]).astype(jnp.bfloat16)
     mask = jnp.repeat(unit_mask, UNIT, axis=1)
-    partial = jnp.stack(
-        [
-            lax.dot_general(
-                tree_rows * mask[which][:, None],
-                tree_rows,
-                (((0,), (0,)), ((), ())),
-                preferred_element_type=jnp.float32,
-            )
-            for which in range(reach[0])
-        ]
-    )
+    packed = []
+    for which in range(reach[0]):
+        full = lax.dot_general(
+            tree_rows * mask[which][:, None],
+            tree_rows,
+            (((0,), (0,)), ((), ())),
+            preferred_element_type=jnp.float32,
+        )
+        packed.append(jnp.concatenate([full[:, :half], full[half:, half:]], axis=0))
+    partial = jnp.stack(packed)
 
     def pick_nodes(level, nodes):
         chosen = touched // 2**level == nodes
         return jnp.sum(jnp.where(chosen[:, None, None], partial, 0.0), axis=0)
 
+    lows = jnp.stack([first_leaf // 2**level for level in range(levels)])
+    highs = jnp.stack([last_leaf // 2**level for level in range(levels)])
+    my_low = jnp.take(lows, device, axis=1)
+    my_high = jnp.take(highs, device, axis=1)
+    spans = [
+        (UNIT * (MINU - 1 + MOSTU) * 2**level - 2 * UNIT) // rows_dev + 1 for level in range(levels)
+    ]
+
+    def gathered(sign, edge, theirs, shared, mine):
+        def moved(value, shift, ids, start):
+            pairs = [(i, i + shift) for i in range(devices - shift)]
+            if sign < 0:
+                pairs = [(j, i) for i, j in pairs]
+            got = lax.ppermute(value, ("row", "col"), pairs)
+            other = device - sign * shift
+            inside = (other >= 0) & (other < devices)
+            named = jnp.take(ids, jnp.clip(other, 0, devices - 1), axis=1)
+            keep = inside & (named == mine)[start:]
+            return jnp.where(keep[:, None, None], got, 0.0)
+
+        total = moved(edge, 1, theirs, 0)
+        covered = 1
+        while covered < min(max(spans), devices - 1):
+            start = sum(span <= covered for span in spans)
+            more = total[start:] + moved(total[start:], covered, shared, start)
+            total = jnp.concatenate([total[:start], more]) if start else more
+            covered *= 2
+        return total
+
+    tails = jnp.stack([pick_nodes(level, my_high[level]) for level in range(levels)])
+    heads = jnp.stack([pick_nodes(level, my_low[level]) for level in range(levels)])
+    to_head = gathered(1, tails, highs, lows, my_low)
+    to_tail = gathered(-1, heads, lows, highs, my_high)
     wanted = []
-    local = LEVELS - 1
-    for level in range(local):
-        group = 2**level
-        low, high = first_leaf // group, last_leaf // group
-        my_low, my_high = jnp.take(low, device), jnp.take(high, device)
-        span = (UNIT * (MINU - 1 + MOSTU) * group - 2 * UNIT) // rows_dev + 1
-        head, tail = pick_nodes(level, my_low), pick_nodes(level, my_high)
-        to_head = jnp.zeros_like(head)
-        to_tail = jnp.zeros_like(head)
-        for shift in range(1, span + 1):
-            up = lax.ppermute(
-                tail, ("row", "col"), [(i, i + shift) for i in range(devices - shift)]
-            )
-            down = lax.ppermute(
-                head, ("row", "col"), [(i + shift, i) for i in range(devices - shift)]
-            )
-            before = jnp.take(high, jnp.maximum(device - shift, 0))
-            behind = jnp.take(low, jnp.minimum(device + shift, devices - 1))
-            use_up = (device >= shift) & (before == my_low)
-            use_down = (device + shift < devices) & (behind == my_high)
-            to_head = to_head + jnp.where(use_up, up, 0.0)
-            to_tail = to_tail + jnp.where(use_down, down, 0.0)
+    for level in range(levels):
         for which in range(reach[level]):
-            node = my_low + which
+            node = my_low[level] + which
             gram = pick_nodes(level, node)
-            gram = gram + jnp.where(node == my_low, to_head, 0.0)
-            wanted.append(gram + jnp.where(node == my_high, to_tail, 0.0))
-    group = 2**local
-    count = leaves // group
-    spread = jnp.stack([pick_nodes(local, node) for node in range(count)])
-    shared = lax.psum(spread, ("row", "col"))
-    for level in range(local, levels):
-        grams = shared.reshape(leaves // 2**level, 2 ** (level - local), width, width).sum(axis=1)
-        index = first // 2**level + jnp.arange(reach[level], dtype=jnp.int32)
-        taken = jnp.take(grams, jnp.minimum(index, leaves // 2**level - 1), axis=0)
-        wanted.extend(taken[which] for which in range(reach[level]))
+            gram = gram + jnp.where(node == my_low[level], to_head[level], 0.0)
+            gram = gram + jnp.where(node == my_high[level], to_tail[level], 0.0)
+            top = jnp.concatenate([gram[:half], gram[half:width].T], axis=1)
+            bottom = jnp.concatenate([gram[half:width], gram[width:]], axis=1)
+            wanted.append(jnp.concatenate([top, bottom], axis=0))
 
     slot = 0
     last = jnp.take(last_leaf, device)
@@ -253,11 +257,33 @@
     pieces = lax.all_to_all(partial_w, "row", split_axis=0, concat_axis=0, tiled=True)
     piece = jnp.sum(pieces.reshape(parts, -1, width).astype(jnp.float32), axis=0)
     sample_w = lax.all_gather(piece.astype(jnp.bfloat16), "row", axis=0, tiled=True)
+    return bases_of(reduce_panels(kernel, sample_w), tree_perm, leaf_units)
+
+
+def reduce_panels(kernel, sample_w):
     columns = lax.axis_size("col")
-    partial = jnp.dot(kernel, sample_w, preferred_element_type=jnp.float32).astype(jnp.bfloat16)
-    pieces = lax.all_to_all(partial, "col", split_axis=0, concat_axis=0, tiled=True)
-    sample = jnp.sum(pieces.reshape(columns, -1, width).astype(jnp.float32), axis=0)
-    return bases_of(sample.astype(jnp.bfloat16), tree_perm, leaf_units)
+    me = lax.axis_index("col")
+    rows_dev = kernel.shape[0] // columns
+    ring = columns // 2
+    place, side = me // 2, me % 2
+    swap = [(i, i ^ 1) for i in range(columns)]
+    ahead = [(i, (i + 2) % columns) for i in range(columns)]
+    owned = []
+    for step in range(ring):
+        target = lax.rem(place + ring - 1 - step, ring)
+        panel = lax.dynamic_slice_in_dim(kernel, target * 2 * rows_dev, 2 * rows_dev)
+        product = jnp.dot(panel, sample_w, preferred_element_type=jnp.float32)
+        lower, upper = product[:rows_dev], product[rows_dev:]
+        theirs = jnp.where(side == 0, upper, lower).astype(jnp.bfloat16)
+        mine = jnp.where(side == 0, lower, upper)
+        owned.append((mine, lax.ppermute(theirs, "col", swap)))
+    total = None
+    for mine, theirs in owned:
+        here = mine + theirs.astype(jnp.float32)
+        if total is not None:
+            here = here + lax.ppermute(total, "col", ahead).astype(jnp.float32)
+        total = here.astype(jnp.bfloat16)
+    return total
 
 
 def solution(mesh):

time: 512 us -> 418 us (0.82)
  waiting for transfers between devices: 241 us -> 108 us
  starting transfers between devices: 35.9 us -> 66.7 us
  blocking collectives: 29.9 us -> 0 us
  other arithmetic: 30 us -> 45.7 us
  between operations: 28.7 us -> 36.8 us
  matrix products: 60 us -> 66.3 us
  local copies, waits for them, and re-layouts: 25.1 us -> 31.3 us
    psum x1 -> x0, waiting for transfers between devices: 115 us -> none  [bases_of(): shared = lax.psum(spread, ('row', 'col'))]
    all_to_all x1, waiting for transfers between devices: 76.7 us -> 14.6 us  [shards(): lax.all_to_all(partial_w, 'row', split_axis=0, concat_axis=0, tiled=True)]
    ppermute x10 -> x17, waiting for transfers between devices: 25.1 us -> 67 us  [the longest x10 43.5 us: moved(): got = lax.ppermute(value, ('row', 'col'), pairs)]
    ppermute x10 -> x17, starting transfers between devices: 27.5 us -> 59.7 us  [the longest x10 52.6 us: moved(): got = lax.ppermute(value, ('row', 'col'), pairs)]
    all_to_all x1 -> x0, blocking collectives: 29.9 us -> none  [shards(): lax.all_to_all(partial_w, 'row', split_axis=0, concat_axis=0, tiled=True)]
    all_to_all x1, waiting for transfers between devices: 0.76 us -> 15.5 us  [to_tree_order(): lax.all_to_all(outgoing, ('row', 'col'), split_axis=0, concat_axis=0, til...]
    all_gather x1, waiting for transfers between devices: 23.8 us -> 10.5 us  [shards(): lax.all_gather(piece.astype(jnp.bfloat16), 'row', axis=0, tiled=True)]
    slice x2 -> x27, local copies, waits for them, and re-layouts: 0.22 us -> 13.5 us  [the longest x9 6.01 us: bases_of(): top = jnp.concatenate([gram[:half], gram[half:width].T], axis=1)]
  transfers between devices with their start and end apart: 14 -> 20, of which waited for: 7 -> 15; matrix products, arithmetic and copies ran while one was open for 4% -> 19% of each run, Pallas kernels for 0% -> 0%
where the time goes in v2:
time: 418 us; the launch traced here: 414 us
  waiting for transfers between devices  108 us (26%)
  starting transfers between devices  66.7 us (16%)
  matrix products  66.3 us (16%)
  Pallas kernels  59.9 us (14%)
  other arithmetic  45.7 us (11%)
  between operations  36.8 us (9%)
  local copies, waits for them, and re-layouts  31.3 us (7%)
    pallas_call x1, Pallas kernels, make_bases(): pl.pallas_call(basis_kernel, out_shape=jax.ShapeDtypeStruct((levels, rows...  59.9 us
    ppermute x10, starting transfers between devices, moved(): got = lax.ppermute(value, ('row', 'col'), pairs)  52.6 us
    ppermute x10, waiting for transfers between devices, moved(): got = lax.ppermute(value, ('row', 'col'), pairs)  43.5 us
    dot_general x4, matrix products, reduce_panels(): product = jnp.dot(panel, sample_w, preferred_element_type=jnp.float32)  35.2 us
    dot_general x1, matrix products, shards(): lax.dot_general(kernel, random_cols, (((0,), (0,)), ((), ())), preferred_...  29.5 us
    all_to_all x1, waiting for transfers between devices, to_tree_order(): lax.all_to_all(outgoing, ('row', 'col'), split_axis=0, concat_axis=0, til...  15.5 us
    all_to_all x1, waiting for transfers between devices, shards(): lax.all_to_all(partial_w, 'row', split_axis=0, concat_axis=0, tiled=True)  14.6 us
    ppermute x3, waiting for transfers between devices, reduce_panels(): here = here + lax.ppermute(total, 'col', ahead).astype(jnp.float32)  12.9 us
  transfers between devices with their start and end apart: 20, of which 15 were waited for; matrix products, arithmetic and copies ran while one was open for 19% of the time, Pallas kernels for 0%

profile of v2, /device:TPU:0, one launch (start us, length us, event | category | flops | bytes accessed | tf_op | source)
XLA Modules:
  0.0 414.4 jit_solution(506457441796540655)
XLA Ops:
  6.5 29.5 %convolution_convert_fusion = bf16[4096,256]{1,0:T(8,128)(2,1)} fusion(bf16[8192,4096]{1,0:T(8,128)(2,1)} %param.6, bf16[8192,256]{1,0:T(8,128)(2,1)} %param.7), kind=kOutput, calls=%fused_computation.10 | convolution fusion | flops 17180917760 | bytes 73400320 | tf_op jit(solution)/shard_map/dot_general | solution.py:254
  36.0 4.4 %all-to-all-start = ((bf16[4,1024,256]{2,1,0:T(8,128)(2,1)}), bf16[4,1024,256]{2,1,0:T(8,128)(2,1)S(1)}, u32[]{:S(2)}, u32[]{:S(2)}) async-start(bf16[4,1024,256]{2,1,0:T(8,128)(2,1)} %bitcast.226), calls=%async_computation | async-start | bytes 4194304 | tf_op jit(solution)/shard_map/all_to_all | solution.py:257
  41.7 9.0 %reduce-window.19 = s32[32,8,128]{2,1,0:T(8,128)S(1)} reduce-window(s32[32,8,128]{2,1,0:T(8,128)S(1)} %fusion.35, s32[]{:T(128)} %constant.438.clone.1), window={size=1x1x128 pad=0_0x0_0x127_0}, to_apply=%region_5.7 | reduce-window | flops 4161536 | bytes 262148 | tf_op jit(solution)/shard_map/reduce-window.1
  51.4 14.6 %all-to-all-done = bf16[4,1024,256]{2,1,0:T(8,128)(2,1)S(1)} async-done(((bf16[4,1024,256]{2,1,0:T(8,128)(2,1)}), bf16[4,1024,256]{2,1,0:T(8,128)(2,1)S(1)}, u32[]{:S(2)}, u32[]{:S(2)}) %all-to-all-start) | async-done | bytes 2097184 | tf_op jit(solution)/shard_map/all_to_all | solution.py:257
  80.6 10.5 %all-gather.2.cloned.1.call-done = bf16[4096,256]{1,0:T(8,128)(2,1)} async-done(((bf16[1024,256]{1,0:T(8,128)(2,1)}), bf16[4096,256]{1,0:T(8,128)(2,1)}) %all-gather.2.cloned.1.call-update) | async-done | bytes 2097168 | tf_op jit(solution)/shard_map/all_gather | solution.py:259
  91.2 10.8 %fusion = f32[2048,256]{1,0:T(8,128)S(1)} fusion(bf16[4096,256]{1,0:T(8,128)(2,1)} %all-gather.2.cloned.1.call-done, bf16[8192,4096]{1,0:T(8,128)(2,1)} %param.6, s32[]{:T(128)S(6)} %select_n.670), kind=kOutput, calls=%fused_computation.2 | convolution fusion | flops 4294967296 | bytes 20971524 | tf_op jit(solution)/shard_map/dot_general | solution.py:275
  103.6 8.1 %fusion.2 = f32[2048,256]{1,0:T(8,128)S(1)} fusion(bf16[4096,256]{1,0:T(8,128)(2,1)S(1)} %copy-done.19, bf16[8192,4096]{1,0:T(8,128)(2,1)} %param.6, s32[]{:T(128)S(6)} %select_n.667), kind=kOutput, calls=%fused_computation.4 | convolution fusion | flops 4294967296 | bytes 20971524 | tf_op jit(solution)/shard_map/dot_general | solution.py:275
  112.5 4.5 %collective-permute-done.3 = bf16[1024,256]{1,0:T(8,128)(2,1)S(1)} collective-permute-done((bf16[1024,256]{1,0:T(8,128)(2,1)S(1)}, bf16[1024,256]{1,0:T(8,128)(2,1)S(1)}, u32[]{:S(2)}, u32[]{:S(2)}) %collective-permute-start.3) | collective-permute-done | bytes 524320 | tf_op jit(solution)/shard_map/ppermute | solution.py:279
  117.1 1.5 collective-permute-start.4
  118.7 8.1 %fusion.4 = f32[2048,256]{1,0:T(8,128)S(1)} fusion(bf16[4096,256]{1,0:T(8,128)(2,1)S(1)} %copy-done.19, bf16[8192,4096]{1,0:T(8,128)(2,1)} %param.6, s32[]{:T(128)S(6)} %select_n.664), kind=kOutput, calls=%fused_computation.6 | convolution fusion | flops 4294967296 | bytes 20971524 | tf_op jit(solution)/shard_map/dot_general | solution.py:275
  128.5 3.0 collective-permute-done.4
  132.0 8.1 %fusion.6 = f32[2048,256]{1,0:T(8,128)S(1)} fusion(bf16[4096,256]{1,0:T(8,128)(2,1)S(1)} %copy-done.19, bf16[8192,4096]{1,0:T(8,128)(2,1)} %param.6, s32[]{:T(128)S(6)} %select_n.661), kind=kOutput, calls=%fused_computation.8 | convolution fusion | flops 4294967296 | bytes 20971524 | tf_op jit(solution)/shard_map/dot_general | solution.py:275
  141.8 3.6 collective-permute-done.5
  145.8 6.1 %collective-permute-done = bf16[1024,256]{1,0:T(8,128)(2,1)S(1)} collective-permute-done((bf16[1024,256]{1,0:T(8,128)(2,1)S(1)}, bf16[1024,256]{1,0:T(8,128)(2,1)S(1)}, u32[]{:S(2)}, u32[]{:S(2)}) %collective-permute-start) | collective-permute-done | bytes 524320 | tf_op jit(solution)/shard_map/ppermute | solution.py:279
  151.9 6.3 %collective-permute-done.6 = bf16[1024,256]{1,0:T(8,128)(2,1)S(1)} collective-permute-done((bf16[1024,256]{1,0:T(8,128)(2,1)S(1)}, bf16[1024,256]{1,0:T(8,128)(2,1)S(1)}, u32[]{:S(2)}, u32[]{:S(2)}) %collective-permute-start.6) | collective-permute-done | bytes 524320 | tf_op jit(solution)/shard_map/ppermute | solution.py:284
  158.4 5.0 %gather_fusion = bf16[1024,256]{1,0:T(8,128)(2,1)} fusion(bf16[1024,256]{1,0:T(8,128)(2,1)S(1)} %add_convert_fusion, s32[1024]{0:T(1024)S(1)} %broadcast_clamp_fusion), kind=kCustom, calls=%fused_computation | custom fusion | bytes 1052672 | tf_op jit(solution)/shard_map/jit(_take)/gather | solution.py:142
  163.4 2.6 all-to-all-start.1
  166.8 15.5 %all-to-all-done.1 = bf16[32,32,256]{2,1,0:T(8,128)(2,1)S(1)} async-done(((bf16[32,32,256]{2,1,0:T(8,128)(2,1)}), bf16[32,32,256]{2,1,0:T(8,128)(2,1)S(1)}, u32[]{:S(2)}, u32[]{:S(2)}) %all-to-all-start.1) | async-done | bytes 524320 | tf_op jit(solution)/shard_map/all_to_all | solution.py:143
  182.3 3.9 gather_fusion.1
  192.4 4.6 %collective-permute-start.7 = (f32[4,384,128]{2,1,0:T(8,128)}, f32[4,384,128]{2,1,0:T(8,128)S(1)}, u32[]{:S(2)}, u32[]{:S(2)}) collective-permute-start(f32[4,384,128]{2,1,0:T(8,128)} %pad_maximum_fusion), channel_id=1, source_target_pairs={{0,1},{1,2},{2,3},{3,4},{4,5},{5,6},{6,7},{7,8},{8,9},{9,10},{10,1... | collective-permute-start | bytes 2359304 | tf_op jit(solution)/shard_map/ppermute | solution.py:202
  197.7 20.1 %collective-permute-done.9 = f32[4,384,128]{2,1,0:T(8,128)S(1)} collective-permute-done((f32[4,384,128]{2,1,0:T(8,128)S(1)}, f32[4,384,128]{2,1,0:T(8,128)S(1)}, u32[]{:S(2)}, u32[]{:S(2)}) %collective-permute-start.9) | collective-permute-done | bytes 786464 | tf_op jit(solution)/shard_map/ppermute | solution.py:202
  220.1 7.0 %collective-permute-done.7 = f32[4,384,128]{2,1,0:T(8,128)S(1)} collective-permute-done((f32[4,384,128]{2,1,0:T(8,128)}, f32[4,384,128]{2,1,0:T(8,128)S(1)}, u32[]{:S(2)}, u32[]{:S(2)}) %collective-permute-start.7) | collective-permute-done | bytes 786464 | tf_op jit(solution)/shard_map/ppermute | solution.py:202
  227.2 5.2 %collective-permute-start.8 = (f32[4,384,128]{2,1,0:T(8,128)S(1)}, f32[4,384,128]{2,1,0:T(8,128)}, u32[]{:S(2)}, u32[]{:S(2)}) collective-permute-start(f32[4,384,128]{2,1,0:T(8,128)S(1)} %broadcast_select_fusion.1), channel_id=1, source_target_pairs={{0,1},{1,2},{2,3},{3,4},{4,5},{5,6},{6,7},{7,8},{8,9},{9,10},{10,1... | collective-permute-start | bytes 2359304 | tf_op jit(solution)/shard_map/ppermute | solution.py:202
  260.5 3.8 collective-permute-done.8
  266.9 9.8 %collective-permute-start.11 = (f32[3,384,128]{2,1,0:T(8,128)}, f32[3,384,128]{2,1,0:T(8,128)}, u32[]{:S(2)}, u32[]{:S(2)}) collective-permute-start(f32[3,384,128]{2,1,0:T(8,128)} %slice.470), channel_id=1, source_target_pairs={{0,2},{1,3},{2,4},{3,5},{4,6},{5,7},{6,8},{7,9},{8,10},{9,11},{10,... | collective-permute-start | bytes 1769480 | tf_op jit(solution)/shard_map/ppermute | solution.py:202
  277.1 8.0 %collective-permute-done.12 = f32[3,384,128]{2,1,0:T(8,128)} collective-permute-done((f32[3,384,128]{2,1,0:T(8,128)}, f32[3,384,128]{2,1,0:T(8,128)}, u32[]{:S(2)}, u32[]{:S(2)}) %collective-permute-start.12) | collective-permute-done | bytes 589856 | tf_op jit(solution)/shard_map/ppermute | solution.py:202
  295.6 1.6 fusion.73
  298.8 17.8 %collective-permute-start.13 = (f32[2,384,128]{2,1,0:T(8,128)}, f32[2,384,128]{2,1,0:T(8,128)S(1)}, u32[]{:S(2)}, u32[]{:S(2)}) collective-permute-start(f32[2,384,128]{2,1,0:T(8,128)} %slice.480), channel_id=1, source_target_pairs={{0,4},{1,5},{2,6},{3,7},{4,8},{5,9},{6,10},{7,11},{8,12},{9,13},{1... | collective-permute-start | bytes 1179656 | tf_op jit(solution)/shard_map/ppermute | solution.py:202
  324.1 1.8 collective-permute-done.13
  328.9 8.8 %collective-permute-start.15 = (f32[1,384,128]{2,1,0:T(8,128)}, f32[1,384,128]{2,1,0:T(8,128)S(1)}, u32[]{:S(2)}, u32[]{:S(2)}) collective-permute-start(f32[1,384,128]{2,1,0:T(8,128)} %slice.490), channel_id=1, source_target_pairs={{0,8},{1,9},{2,10},{3,11},{4,12},{5,13},{6,14},{7,15},{8,16},{9,17... | collective-permute-start | bytes 589832 | tf_op jit(solution)/shard_map/ppermute | solution.py:202
  338.8 2.1 bitcast_add_fusion
  347.6 59.9 %shard_map.46 = bf16[4,1024,256]{2,1,0:T(8,128)(2,1)} custom-call(s32[32]{0:T(128)S(1)} %pad_add_fusion.2.index_ref, f32[9,256,256]{2,1,0:T(8,128)S(1)} %fusion.24.gram_ref, bf16[1024,256]{1,0:T(8,128)(2,1)S(1)} %gather_fusion.1), custom_call_target="tpu_custom_call" | custom-call | tf_op jit(solution)/shard_map/pallas_call | solution.py:112
  (222 shorter events, 71.8 us)
Async XLA Ops:
  36.0 30.0 %all-to-all-start = ((bf16[4,1024,256]{2,1,0:T(8,128)(2,1)}), bf16[4,1024,256]{2,1,0:T(8,128)(2,1)S(1)}, u32[]{:S(2)}, u32[]{:S(2)}) async-start(bf16[4,1024,256]{2,1,0:T(8,128)(2,1)} %bitcast.226), calls=%async_computation | async-start | bytes 4194304 | tf_op jit(solution)/shard_map/all_to_all | solution.py:257
  40.4 50.8 %all-gather.2.cloned.1.call-start = ((), (), s32[]{:S(2)}) async-start(), calls=%async_computation.2 | async-start | bytes 2621440 | tf_op jit(solution)/shard_map/all_gather | solution.py:259
  91.2 12.4 %copy-start.19 = (bf16[4096,256]{1,0:T(8,128)(2,1)S(1)}, bf16[4096,256]{1,0:T(8,128)(2,1)}, u32[]{:S(2)}) copy-start(bf16[4096,256]{1,0:T(8,128)(2,1)} %all-gather.2.cloned.1.call-done) | copy-start | bytes 6291460
  102.1 14.9 %collective-permute-start.3 = (bf16[1024,256]{1,0:T(8,128)(2,1)S(1)}, bf16[1024,256]{1,0:T(8,128)(2,1)S(1)}, u32[]{:S(2)}, u32[]{:S(2)}) collective-permute-start(bf16[1024,256]{1,0:T(8,128)(2,1)S(1)} %select_convert_fusion), channel_id=1, source_target_pairs={{0,1},{1,0},{2,3},{3,2},{4,5},{5,4},{6,7},{7,6},{8,9},{9,8},{10,11... | collective-permute-start | bytes 1572872 | tf_op jit(solution)/shard_map/ppermute | solution.py:279
  111.8 16.6 %collective-permute-start.2 = (bf16[1024,256]{1,0:T(8,128)(2,1)S(1)}, bf16[1024,256]{1,0:T(8,128)(2,1)S(1)}, u32[]{:S(2)}, u32[]{:S(2)}) collective-permute-start(bf16[1024,256]{1,0:T(8,128)(2,1)S(1)} %select_convert_fusion.1), channel_id=1, source_target_pairs={{0,1},{1,0},{2,3},{3,2},{4,5},{5,4},{6,7},{7,6},{8,9},{9,8},{10,11... | collective-permute-start | bytes 1572872 | tf_op jit(solution)/shard_map/ppermute | solution.py:279
  117.1 14.3 %collective-permute-start.4 = (bf16[1024,256]{1,0:T(8,128)(2,1)S(1)}, bf16[1024,256]{1,0:T(8,128)(2,1)S(1)}, u32[]{:S(2)}, u32[]{:S(2)}) collective-permute-start(bf16[1024,256]{1,0:T(8,128)(2,1)S(1)} %add_convert_fusion.3), channel_id=1, source_target_pairs={{0,2},{1,3},{2,4},{3,5},{4,6},{5,7},{6,0},{7,1},{8,10},{9,11},{10,... | collective-permute-start | bytes 1572872 | tf_op jit(solution)/shard_map/ppermute | solution.py:284
  126.9 14.8 %collective-permute-start.1 = (bf16[1024,256]{1,0:T(8,128)(2,1)S(1)}, bf16[1024,256]{1,0:T(8,128)(2,1)S(1)}, u32[]{:S(2)}, u32[]{:S(2)}) collective-permute-start(bf16[1024,256]{1,0:T(8,128)(2,1)S(1)} %select_convert_fusion.2), channel_id=1, source_target_pairs={{0,1},{1,0},{2,3},{3,2},{4,5},{5,4},{6,7},{7,6},{8,9},{9,8},{10,11... | collective-permute-start | bytes 1572872 | tf_op jit(solution)/shard_map/ppermute | solution.py:279
  131.7 13.7 %collective-permute-start.5 = (bf16[1024,256]{1,0:T(8,128)(2,1)S(1)}, bf16[1024,256]{1,0:T(8,128)(2,1)S(1)}, u32[]{:S(2)}, u32[]{:S(2)}) collective-permute-start(bf16[1024,256]{1,0:T(8,128)(2,1)S(1)} %add_convert_fusion.2), channel_id=1, source_target_pairs={{0,2},{1,3},{2,4},{3,5},{4,6},{5,7},{6,0},{7,1},{8,10},{9,11},{10,... | collective-permute-start | bytes 1572872 | tf_op jit(solution)/shard_map/ppermute | solution.py:284
  140.2 11.7 %collective-permute-start = (bf16[1024,256]{1,0:T(8,128)(2,1)S(1)}, bf16[1024,256]{1,0:T(8,128)(2,1)S(1)}, u32[]{:S(2)}, u32[]{:S(2)}) collective-permute-start(bf16[1024,256]{1,0:T(8,128)(2,1)S(1)} %select_convert_fusion.3), channel_id=1, source_target_pairs={{0,1},{1,0},{2,3},{3,2},{4,5},{5,4},{6,7},{7,6},{8,9},{9,8},{10,11... | collective-permute-start | bytes 1572872 | tf_op jit(solution)/shard_map/ppermute | solution.py:279
  145.6 12.6 %collective-permute-start.6 = (bf16[1024,256]{1,0:T(8,128)(2,1)S(1)}, bf16[1024,256]{1,0:T(8,128)(2,1)S(1)}, u32[]{:S(2)}, u32[]{:S(2)}) collective-permute-start(bf16[1024,256]{1,0:T(8,128)(2,1)S(1)} %add_convert_fusion.1), channel_id=1, source_target_pairs={{0,2},{1,3},{2,4},{3,5},{4,6},{5,7},{6,0},{7,1},{8,10},{9,11},{10,... | collective-permute-start | bytes 1572872 | tf_op jit(solution)/shard_map/ppermute | solution.py:284
  163.4 18.8 %all-to-all-start.1 = ((bf16[32,32,256]{2,1,0:T(8,128)(2,1)}), bf16[32,32,256]{2,1,0:T(8,128)(2,1)S(1)}, u32[]{:S(2)}, u32[]{:S(2)}) async-start(bf16[32,32,256]{2,1,0:T(8,128)(2,1)} %bitcast.9), calls=%async_computation.1 | async-start | bytes 1048576 | tf_op jit(solution)/shard_map/all_to_all | solution.py:143
  189.3 28.5 %collective-permute-start.9 = (f32[4,384,128]{2,1,0:T(8,128)S(1)}, f32[4,384,128]{2,1,0:T(8,128)S(1)}, u32[]{:S(2)}, u32[]{:S(2)}) collective-permute-start(f32[4,384,128]{2,1,0:T(8,128)S(1)} %pad_maximum_fusion.1), channel_id=1, source_target_pairs={{1,0},{2,1},{3,2},{4,3},{5,4},{6,5},{7,6},{8,7},{9,8},{10,9},{11,1... | collective-permute-start | bytes 2359304 | tf_op jit(solution)/shard_map/ppermute | solution.py:202
  191.5 62.4 %copy-start.14 = (pred[4]{0:T(512)(128)(4,1)S(1)}, pred[4]{0:T(512)(128)(4,1)}, u32[]{:S(2)}) copy-start(pred[4]{0:T(512)(128)(4,1)} %get-tuple-element.215) | copy-start | bytes 16
  192.4 34.6 %collective-permute-start.7 = (f32[4,384,128]{2,1,0:T(8,128)}, f32[4,384,128]{2,1,0:T(8,128)S(1)}, u32[]{:S(2)}, u32[]{:S(2)}) collective-permute-start(f32[4,384,128]{2,1,0:T(8,128)} %pad_maximum_fusion), channel_id=1, source_target_pairs={{0,1},{1,2},{2,3},{3,4},{4,5},{5,6},{6,7},{7,8},{8,9},{9,10},{10,1... | collective-permute-start | bytes 2359304 | tf_op jit(solution)/shard_map/ppermute | solution.py:202
  197.7 56.9 %copy-start.15 = (pred[4]{0:T(512)(128)(4,1)S(1)}, pred[4]{0:T(512)(128)(4,1)}, u32[]{:S(2)}) copy-start(pred[4]{0:T(512)(128)(4,1)} %get-tuple-element.210) | copy-start | bytes 16
  218.8 38.1 %collective-permute-start.10 = (f32[4,384,128]{2,1,0:T(8,128)}, f32[4,384,128]{2,1,0:T(8,128)}, u32[]{:S(2)}, u32[]{:S(2)}) collective-permute-start(f32[4,384,128]{2,1,0:T(8,128)} %broadcast_select_fusion), channel_id=1, source_target_pairs={{1,0},{2,1},{3,2},{4,3},{5,4},{6,5},{7,6},{8,7},{9,8},{10,9},{11,1... | collective-permute-start | bytes 2359304 | tf_op jit(solution)/shard_map/ppermute | solution.py:202
  227.2 37.1 %collective-permute-start.8 = (f32[4,384,128]{2,1,0:T(8,128)S(1)}, f32[4,384,128]{2,1,0:T(8,128)}, u32[]{:S(2)}, u32[]{:S(2)}) collective-permute-start(f32[4,384,128]{2,1,0:T(8,128)S(1)} %broadcast_select_fusion.1), channel_id=1, source_target_pairs={{0,1},{1,2},{2,3},{3,4},{4,5},{5,6},{6,7},{7,8},{8,9},{9,10},{10,1... | collective-permute-start | bytes 2359304 | tf_op jit(solution)/shard_map/ppermute | solution.py:202
  258.3 8.3 %copy-start = (f32[4,384,128]{2,1,0:T(8,128)}, f32[4,384,128]{2,1,0:T(8,128)S(1)}, u32[]{:S(2)}) copy-start(f32[4,384,128]{2,1,0:T(8,128)S(1)} %select_add_fusion) | copy-start | bytes 2359300
  259.2 26.0 %collective-permute-start.12 = (f32[3,384,128]{2,1,0:T(8,128)}, f32[3,384,128]{2,1,0:T(8,128)}, u32[]{:S(2)}, u32[]{:S(2)}) collective-permute-start(f32[3,384,128]{2,1,0:T(8,128)} %slice.472), channel_id=1, source_target_pairs={{2,0},{3,1},{4,2},{5,3},{6,4},{7,5},{8,6},{9,7},{10,8},{11,9},{12,... | collective-permute-start | bytes 1769480 | tf_op jit(solution)/shard_map/ppermute | solution.py:202
  266.7 18.5 %copy-start.18 = (pred[3]{0:T(512)(128)(4,1)S(1)}, pred[3]{0:T(512)(128)(4,1)}, u32[]{:S(2)}) copy-start(pred[3]{0:T(512)(128)(4,1)} %slice_and_fusion.2) | copy-start | bytes 13
  266.9 23.0 %collective-permute-start.11 = (f32[3,384,128]{2,1,0:T(8,128)}, f32[3,384,128]{2,1,0:T(8,128)}, u32[]{:S(2)}, u32[]{:S(2)}) collective-permute-start(f32[3,384,128]{2,1,0:T(8,128)} %slice.470), channel_id=1, source_target_pairs={{0,2},{1,3},{2,4},{3,5},{4,6},{5,7},{6,8},{7,9},{8,10},{9,11},{10,... | collective-permute-start | bytes 1769480 | tf_op jit(solution)/shard_map/ppermute | solution.py:202
  276.9 13.0 %copy-start.2 = (f32[4,384,128]{2,1,0:T(8,128)S(1)}, f32[4,384,128]{2,1,0:T(8,128)}, u32[]{:S(2)}) copy-start(f32[4,384,128]{2,1,0:T(8,128)} %copy-done.1) | copy-start | bytes 2359300
  276.9 13.0 %copy-start.17 = (pred[3]{0:T(512)(128)(4,1)S(1)}, pred[3]{0:T(512)(128)(4,1)}, u32[]{:S(2)}) copy-start(pred[3]{0:T(512)(128)(4,1)} %slice_and_fusion.3) | copy-start | bytes 13
  277.1 14.9 %copy-start.7 = (f32[384,128]{1,0:T(8,128)S(1)}, f32[384,128]{1,0:T(8,128)}, u32[]{:S(2)}) copy-start(f32[384,128]{1,0:T(8,128)} %copy-done.6) | copy-start | bytes 589828
  277.1 14.9 %copy-start.12 = (f32[384,128]{1,0:T(8,128)S(1)}, f32[384,128]{1,0:T(8,128)}, u32[]{:S(2)}) copy-start(f32[384,128]{1,0:T(8,128)} %get-tuple-element.146) | copy-start | bytes 589828
  287.3 33.6 %collective-permute-start.14 = (f32[2,384,128]{2,1,0:T(8,128)}, f32[2,384,128]{2,1,0:T(8,128)}, u32[]{:S(2)}, u32[]{:S(2)}) collective-permute-start(f32[2,384,128]{2,1,0:T(8,128)} %slice.482), channel_id=1, source_target_pairs={{4,0},{5,1},{6,2},{7,3},{8,4},{9,5},{10,6},{11,7},{12,8},{13,9},{1... | collective-permute-start | bytes 1179656 | tf_op jit(solution)/shard_map/ppermute | solution.py:202
  297.9 28.0 %copy-start.4 = (f32[3,384,128]{2,1,0:T(8,128)S(1)}, f32[3,384,128]{2,1,0:T(8,128)}, u32[]{:S(2)}) copy-start(f32[3,384,128]{2,1,0:T(8,128)} %copy-done.3) | copy-start | bytes 1769476
  298.8 27.0 %collective-permute-start.13 = (f32[2,384,128]{2,1,0:T(8,128)}, f32[2,384,128]{2,1,0:T(8,128)S(1)}, u32[]{:S(2)}, u32[]{:S(2)}) collective-permute-start(f32[2,384,128]{2,1,0:T(8,128)} %slice.480), channel_id=1, source_target_pairs={{0,4},{1,5},{2,6},{3,7},{4,8},{5,9},{6,10},{7,11},{8,12},{9,13},{1... | collective-permute-start | bytes 1179656 | tf_op jit(solution)/shard_map/ppermute | solution.py:202
  316.6 10.1 %copy-start.9 = (f32[384,128]{1,0:T(8,128)S(1)}, f32[384,128]{1,0:T(8,128)}, u32[]{:S(2)}) copy-start(f32[384,128]{1,0:T(8,128)} %copy-done.8) | copy-start | bytes 589828
  322.1 16.7 %copy-start.11 = (f32[384,128]{1,0:T(8,128)S(1)}, f32[384,128]{1,0:T(8,128)}, u32[]{:S(2)}) copy-start(f32[384,128]{1,0:T(8,128)} %copy-done.10) | copy-start | bytes 589828
  322.8 16.0 %collective-permute-start.16 = (f32[1,384,128]{2,1,0:T(8,128)}, f32[1,384,128]{2,1,0:T(8,128)}, u32[]{:S(2)}, u32[]{:S(2)}) collective-permute-start(f32[1,384,128]{2,1,0:T(8,128)} %slice.491), channel_id=1, source_target_pairs={{8,0},{9,1},{10,2},{11,3},{12,4},{13,5},{14,6},{15,7},{16,8},{17,9... | collective-permute-start | bytes 589832 | tf_op jit(solution)/shard_map/ppermute | solution.py:202
  328.9 9.8 %collective-permute-start.15 = (f32[1,384,128]{2,1,0:T(8,128)}, f32[1,384,128]{2,1,0:T(8,128)S(1)}, u32[]{:S(2)}, u32[]{:S(2)}) collective-permute-start(f32[1,384,128]{2,1,0:T(8,128)} %slice.490), channel_id=1, source_target_pairs={{0,8},{1,9},{2,10},{3,11},{4,12},{5,13},{6,14},{7,15},{8,16},{9,17... | collective-permute-start | bytes 589832 | tf_op jit(solution)/shard_map/ppermute | solution.py:202
  (9 other events, 32.1 us)
Sparse Core Ops, SparseCore 0:
  67.5 23.6 all-gather.1
